TPU v7x, 32 devices: a whole 2x2x4 slice. The times are simulated.
32 devices in a mesh: frame: 4 (over y, x), height: 2 (over core), width: 4 (over z).
Axes of the slice: x: 2, y: 2, z: 4, core: 2. Of those that a mesh axis runs over, the one named last changes fastest.
Arguments:
- tokens: bfloat16 [4, 16, 8, 16, 1536], P('frame', None, 'height', 'width'), may hold values from -6 to 6
- qkv_weight: bfloat16 [3, 768, 1536], P(None, ('frame', 'height')), may hold values from -0.15625 to 0.15625
- tile_mask: int32 [4, 4, 2, 4], P('frame'), may hold values 0 or 1
Outputs:
- attended: bfloat16 [4, 16, 8, 16, 768], P('frame', None, 'height', 'width')
Inputs may be any that keep to these rules, and one draw needn't show every extreme that they name: `tile_mask`: selection flag of each tile.
All inputs are finite; a program needn't handle non-finite values. No bound on the sum of `tile_mask` on one device may be relied on, other than what follows from the above.
Results may differ from a plain program's by a relative error of at most 0.0082.
Values may be sent and summed in bfloat16 or wider, within the bound.
A program may use at most 64 MiB of HBM per device.

v0:
```python
import functools
import math

import jax
import jax.numpy as jnp
from jax import lax
from jax.experimental import pallas as pl
from jax.experimental.pallas import tpu as pltpu
from jax.sharding import PartitionSpec as P

HEAD_DIM = 128
TILE = 4
CUBE = TILE * TILE * TILE
MESH = pl.DeviceIdType.MESH

epsilon = 1e-06


def kernel(
    n_h, n_w, x_ref, w_ref, tm_ref, o_ref,
    xs, xn, w_all, kbuf, vbuf, qbuf, mask,
    loc_sem, tok_s, tok_r, own_s, own_r, fwd_s, fwd_r, hgt_s, hgt_r, kvx_s, kvx_r,
):
    f, h, w = lax.axis_index("frame"), lax.axis_index("height"), lax.axis_index("width")
    f1 = f + 1 - 2 * (f % 2)
    f2 = f + 2 - 4 * ((f // 2) % 2)
    rows = w_ref.shape[1]
    features = w_ref.shape[2]
    half = features // 2
    tokens = xn.shape[0] // 3
    heads = kbuf.shape[2]
    slots = kbuf.shape[1]
    key, value, query = 1, 2, 0

    def row(parity, height):
        return pl.ds(pl.multiple_of((parity * n_h + height) * rows, rows), rows)

    parity = f % 2
    mine, beside = row(parity, h), row(1 - parity, h)

    def remote(src, dst, send, recv, target):
        return pltpu.make_async_remote_copy(
            src_ref=src, dst_ref=dst, send_sem=send, recv_sem=recv,
            device_id=target, device_id_type=MESH,
        )

    def to_frame(i):
        return ((f1, f2)[i], h, w)

    def own_copy(s, p, i):
        cols = pl.ds(p * half, half)
        return remote(
            w_ref.at[s, :, cols], w_all.at[s, i, mine, cols], own_s.at[s, p, i], own_r.at[s, p, i], to_frame(i)
        )

    def fwd_copy(s, i):
        cols = pl.ds(0, half) if i == 1 else pl.ds(half, half)
        src = w_all.at[s, 0, beside, cols] if i == 1 else w_all.at[s, 1, mine, cols]
        dst = w_all.at[s, 1, beside if i == 1 else mine, cols]
        return remote(src, dst, fwd_s.at[s, i], fwd_r.at[s, i], to_frame(i))

    piece_at = ((0, mine), (0, beside), (1, mine), (1, beside))

    def hgt_copy(s, piece, d):
        group, place = piece_at[piece]
        dst = w_all.at[s, group, place]
        src = w_ref.at[s] if piece == 0 else dst
        target = (f, lax.rem(h + d, n_h), w)
        return remote(src, dst, hgt_s.at[s, piece, d - 1], hgt_r.at[s, piece, d - 1], target)

    def kv_copy(g, which, up):
        buf = (kbuf, vbuf)[which]
        slot = 1 if up or n_h == 2 else 2
        target = (f, h + 1 if up else h - 1, w)
        e = 0 if up else 1
        return remote(buf.at[g, 0], buf.at[g, slot], kvx_s.at[g, which, e], kvx_r.at[g, which, e], target)

    def tok_copy(e):
        target = (f, h, w + 1 if e == 0 else w - 1)
        return remote(x_ref.at[0], xs.at[1 if e == 0 else 2], tok_s.at[e], tok_r.at[e], target)

    local_x = pltpu.make_async_copy(x_ref.at[0], xs.at[0], loc_sem.at[0])
    local_w = [
        pltpu.make_async_copy(w_ref.at[s], w_all.at[s, 0, mine], loc_sem.at[1 + s]) for s in range(3)
    ]
    local_x.start()
    for s in range(3):
        local_w[s].start()

    has_left, has_right = w > 0, w < n_w - 1
    has_below, has_above = h > 0, h < n_h - 1

    barrier = pltpu.get_barrier_semaphore()

    def greet(target):
        pl.semaphore_signal(barrier, inc=1, device_id=target, device_id_type=MESH)

    greet(to_frame(0))
    greet(to_frame(1))
    for d in range(1, n_h):
        greet((f, lax.rem(h + d, n_h), w))

    @pl.when(has_left)
    def _():
        greet((f, h, w - 1))

    @pl.when(has_right)
    def _():
        greet((f, h, w + 1))

    peers = n_h + 1 + has_left.astype(jnp.int32) + has_right.astype(jnp.int32)
    pl.semaphore_wait(barrier, peers)

    def send_own(s, p):
        own_copy(s, p, 0).start()
        own_copy(s, p, 1).start()

    def wait_own(s, p):
        own_copy(s, p, 0).wait_recv()
        own_copy(s, p, 1).wait_recv()

    def send_fwd(s):
        fwd_copy(s, 0).start()
        fwd_copy(s, 1).start()

    def relay(s, *pieces):
        for piece in pieces:
            for d in range(1, n_h):
                hgt_copy(s, piece, d).start()

    def take_fwd(s):
        fwd_copy(s, 0).wait_recv()
        fwd_copy(s, 1).wait_recv()
        relay(s, 3)

    send_own(key, 0)
    send_own(key, 1)

    @pl.when(has_right)
    def _():
        tok_copy(0).start()

    @pl.when(has_left)
    def _():
        tok_copy(1).start()

    for s in (key, value, query):
        relay(s, 0)

    q_tile = lax.broadcasted_iota(jnp.int32, (tokens, tokens), 0) // CUBE
    k_tile = lax.broadcasted_iota(jnp.int32, (tokens, tokens), 1) // CUBE
    near = jnp.abs(q_tile - k_tile) <= 1
    same = q_tile == k_tile
    total_h, total_w = tm_ref.shape[2], tm_ref.shape[3]
    for b in range(slots):
        if b == 0:
            row_h = h
        elif n_h == 2:
            row_h = 1 - h
        else:
            row_h = h - 1 if b == 1 else h + 1
        for c in range(3):
            col_w = w + (0, -1, 1)[c]
            inside = ((row_h >= 0) & (row_h < total_h) & (col_w >= 0) & (col_w < total_w)).astype(jnp.int32)
            at_h = jnp.minimum(jnp.maximum(row_h, 0), total_h - 1)
            at_w = jnp.minimum(jnp.maximum(col_w, 0), total_w - 1)
            flags = jnp.zeros((tokens, tokens), jnp.int32)
            for t in range(tokens // CUBE):
                flag = tm_ref[0, t, at_h, at_w] * inside
                flags = jnp.where(k_tile == t, flag, flags)
            seen = flags == 1
            if b == 0 and c == 0:
                seen = seen | same
            allowed = jnp.where(near & seen, jnp.float32(1.0), jnp.float32(0.0))
            mask[b, :, c * tokens : (c + 1) * tokens] = allowed.astype(jnp.bfloat16)

    def normalise(c):
        step = 64
        for t in range(tokens // step):
            frames = step // (TILE * TILE)
            block = xs[c, t * frames : (t + 1) * frames].astype(jnp.float32).reshape(step, features)
            scale = lax.rsqrt(jnp.mean(block * block, -1, keepdims=True) + epsilon)
            xn[c * tokens + t * step : c * tokens + (t + 1) * step, :] = (block * scale).astype(jnp.bfloat16)

    def blank(c):
        xn[c * tokens : (c + 1) * tokens, :] = jnp.zeros((tokens, features), jnp.bfloat16)

    def head_norm(raw):
        return (raw * lax.rsqrt(jnp.mean(raw * raw, -1, keepdims=True) + epsilon)).astype(jnp.bfloat16)

    contract_last = (((1,), (1,)), ((), ()))

    def project_kv(g, s, sides):
        buf = kbuf if s == key else vbuf

        at = {0: pl.ds(0, tokens), 1: pl.ds(tokens, 2 * tokens), 2: pl.ds(0, 3 * tokens)}[sides]
        raw = lax.dot_general(xn[at, :], w_all[s, g], contract_last, preferred_element_type=jnp.float32)
        for j in range(heads):
            part = raw[:, j * HEAD_DIM : (j + 1) * HEAD_DIM]
            buf[g, 0, j, at, :] = head_norm(part) if s == key else part.astype(jnp.bfloat16)
        if not sides:
            return

        which = 0 if s == key else 1

        @pl.when(has_above)
        def _():
            kv_copy(g, which, True).start()

        @pl.when(has_below)
        def _():
            kv_copy(g, which, False).start()

    def project_q(g, first, count):
        place = pl.ds(pl.multiple_of(first * HEAD_DIM, HEAD_DIM), count * HEAD_DIM)
        raw = lax.dot_general(
            xn[0:tokens, :], w_all[query, g, place], contract_last, preferred_element_type=jnp.float32
        )
        for j in range(count):
            qbuf[g, first + j] = head_norm(raw[:, j * HEAD_DIM : (j + 1) * HEAD_DIM])

    def wait_kv(g):
        for which in range(2):
            @pl.when(has_below)
            def _():
                kv_copy(g, which, True).wait_recv()

            @pl.when(has_above)
            def _():
                kv_copy(g, which, False).wait_recv()

    def wait_hgt(s, pieces):
        for piece in pieces:
            for d in range(1, n_h):
                hgt_copy(s, piece, d).wait_recv()

    factor = HEAD_DIM ** (-0.5) * math.log2(math.e)
    ones = jnp.ones((3 * tokens, HEAD_DIM), jnp.bfloat16)

    def attend(g, first, count):
        pair = f // 2
        base = (pair if g == 0 else 1 - pair) * heads

        def body(i, carry):
            j = first + i
            q = qbuf[g, j]
            total = jnp.zeros((tokens, 2 * HEAD_DIM), jnp.float32)
            for b in range(slots):
                scores = lax.dot_general(q, kbuf[g, b, j], contract_last, preferred_element_type=jnp.float32)
                weight = jnp.exp2(scores * factor).astype(jnp.bfloat16) * mask[b]
                wide = jnp.concatenate([vbuf[g, b, j], ones], 1)
                total = total + jnp.dot(weight, wide, preferred_element_type=jnp.float32)
            result = (total[:, :HEAD_DIM] / total[:, HEAD_DIM:]).astype(o_ref.dtype)
            lanes = pl.ds(pl.multiple_of((base + j) * HEAD_DIM, HEAD_DIM), HEAD_DIM)
            o_ref[:, lanes] = result
            return carry

        lax.fori_loop(0, count, body, 0)

    if n_h > 2:
        for edge, slot in ((h == 0, 1), (h == n_h - 1, 2)):
            @pl.when(edge)
            def _():
                for g in range(2):
                    kbuf[g, slot] = jnp.zeros(kbuf.shape[2:], jnp.bfloat16)
                    vbuf[g, slot] = jnp.zeros(vbuf.shape[2:], jnp.bfloat16)

    local_x.wait()
    normalise(0)
    wait_own(key, 0)
    send_own(value, 0)
    fwd_copy(key, 1).start()
    wait_own(key, 1)
    fwd_copy(key, 0).start()
    relay(key, 1, 2)
    wait_own(value, 0)
    send_own(value, 1)
    local_w[key].wait()
    wait_hgt(key, (0, 1))
    project_kv(0, key, 0)
    take_fwd(key)
    send_own(query, 0)
    wait_hgt(key, (2, 3))
    project_kv(1, key, 0)
    wait_own(value, 1)
    send_own(query, 1)
    relay(value, 1, 2)
    @pl.when(has_left)
    def _():
        tok_copy(0).wait_recv()
        normalise(1)

    @pl.when(w == 0)
    def _():
        blank(1)

    @pl.when(has_right)
    def _():
        tok_copy(1).wait_recv()
        normalise(2)

    @pl.when(w == n_w - 1)
    def _():
        blank(2)

    project_kv(0, key, 1)
    wait_own(query, 0)
    send_fwd(value)
    local_w[value].wait()
    wait_hgt(value, (0, 1))
    project_kv(0, value, 2)
    wait_own(query, 1)
    send_fwd(query)
    relay(query, 1, 2)
    project_kv(1, key, 1)
    early = n_h * rows // HEAD_DIM
    local_w[query].wait()
    wait_hgt(query, (0, 1))
    project_q(0, 0, heads)
    wait_hgt(query, (2,))
    project_q(1, parity * (heads - early), early)
    wait_kv(0)
    attend(0, 0, heads)
    take_fwd(value)
    wait_hgt(value, (2, 3))
    project_kv(1, value, 2)
    take_fwd(query)
    wait_kv(1)
    attend(1, parity * (heads - early), early)
    wait_hgt(query, (3,))
    project_q(1, (1 - parity) * early, heads - early)
    attend(1, (1 - parity) * early, heads - early)

    for s in range(3):
        for i in range(2):
            own_copy(s, 0, i).wait_send()
            own_copy(s, 1, i).wait_send()
            fwd_copy(s, i).wait_send()
        for piece in range(4):
            for d in range(1, n_h):
                hgt_copy(s, piece, d).wait_send()

    @pl.when(has_right)
    def _():
        tok_copy(0).wait_send()

    @pl.when(has_left)
    def _():
        tok_copy(1).wait_send()

    for g in range(2):
        for which in range(2):
            @pl.when(has_above)
            def _():
                kv_copy(g, which, True).wait_send()

            @pl.when(has_below)
            def _():
                kv_copy(g, which, False).wait_send()


def per_device(n_f, n_h, n_w, tokens, qkv_weight, tile_mask):
    clips, frames, rows, columns, features = tokens.shape
    count = frames * rows * columns
    width = qkv_weight.shape[1] * n_f * n_h
    if n_f != 4 or n_h < 2 or clips != 1 or rows != TILE or columns != TILE:
        raise ValueError("unsupported placement")
    heads = width // HEAD_DIM // 2
    slots = 2 if n_h == 2 else 3
    dma = pltpu.SemaphoreType.DMA
    out = pl.pallas_call(
        functools.partial(kernel, n_h, n_w),
        out_shape=jax.ShapeDtypeStruct((count, width), jnp.bfloat16),
        in_specs=[
            pl.BlockSpec(memory_space=pl.ANY),
            pl.BlockSpec(memory_space=pl.ANY),
            pl.BlockSpec(memory_space=pltpu.SMEM),
        ],
        out_specs=pl.BlockSpec(memory_space=pltpu.VMEM),
        scratch_shapes=[
            pltpu.VMEM((3, frames, rows, columns, features), jnp.bfloat16),
            pltpu.VMEM((3 * count, features), jnp.bfloat16),
            pltpu.VMEM((3, 2, width // 2, features), jnp.bfloat16),
            pltpu.VMEM((2, slots, heads, 3 * count, HEAD_DIM), jnp.bfloat16),
            pltpu.VMEM((2, slots, heads, 3 * count, HEAD_DIM), jnp.bfloat16),
            pltpu.VMEM((2, heads, count, HEAD_DIM), jnp.bfloat16),
            pltpu.VMEM((slots, count, 3 * count), jnp.bfloat16),
            dma((4,)), dma((2,)), dma((2,)), dma((3, 2, 2)), dma((3, 2, 2)), dma((3, 2)), dma((3, 2)),
            dma((3, 4, n_h - 1)), dma((3, 4, n_h - 1)), dma((2, 2, 2)), dma((2, 2, 2)),
        ],
        compiler_params=pltpu.CompilerParams(
            collective_id=0, has_side_effects=True, vmem_limit_bytes=56 << 20
        ),
    )(tokens, qkv_weight, tile_mask)
    return out.reshape(clips, frames, rows, columns, width)


def solution(mesh):
    in_specs = (
        P("frame", None, "height", "width", None),
        P(None, ("frame", "height"), None),
        P("frame", None, None, None),
    )
    out_specs = P("frame", None, "height", "width", None)
    body = functools.partial(
        per_device, mesh.shape["frame"], mesh.shape["height"], mesh.shape["width"]
    )
    return jax.shard_map(body, mesh=mesh, in_specs=in_specs, out_specs=out_specs, check_vma=False)
```

profile of v0, /device:TPU:0, one launch (start us, length us, event | category | flops | bytes accessed | tf_op | source)
XLA Modules:
  0.0 45.6 jit_solution(2869001638361698882)
XLA Ops:
  0.0 43.8 %shard_map.37 = bf16[256,768]{1,0:T(8,128)(2,1)} custom-call(bf16[1,16,4,4,1536]{4,3,2,1,0:T(4,128)(2,1)} %x_ref.1, bf16[3,96,1536]{2,1,0:T(8,128)(2,1)} %w_ref.1, s32[1,4,2,4]{3,2,1,0:T(2,128)} %tm_ref.1), custom_call_target="tpu_custom_call" | custom-call | tf_op jit(solution)/shard_map/pallas_call | solution.py:371
  43.8 1.8 %reshape.3 = bf16[1,16,4,4,768]{4,3,2,1,0:T(4,128)(2,1)} reshape(bf16[256,768]{1,0:T(8,128)(2,1)} %shard_map.37) | data formatting | bytes 786432 | tf_op jit(solution)/shard_map/reshape | solution.py:395
where the time goes:
time: 45.8 us; the launch traced here: 45.6 us
  Pallas kernels  43.8 us (96%)
  local copies, waits for them, and re-layouts  1.84 us (4%)
    pallas_call x1, Pallas kernels, per_device(): pl.pallas_call(functools.partial(kernel, n_h, n_w), out_shape=jax.ShapeDt...  43.8 us
    reshape x1, local copies, waits for them, and re-layouts, per_device(): return out.reshape(clips, frames, rows, columns, width)  1.84 us

commit v1 on v0

v1 whole, which is shorter than its diff:
```python
import functools
import math

import jax
import jax.numpy as jnp
from jax import lax
from jax.experimental import pallas as pl
from jax.experimental.pallas import tpu as pltpu
from jax.sharding import PartitionSpec as P

HEAD_DIM = 128
TILE = 4
VMEM_LIMIT = 54472 << 10
CUBE = TILE * TILE * TILE
MESH = pl.DeviceIdType.MESH

epsilon = 1e-06
QUERY, KEY, VALUE = 0, 1, 2


def kernel(
    n_h, n_w, x_ref, w_ref, tm_ref, o_ref,
    xs, xn, w_all, kbuf, vbuf, qbuf, mask,
    loc_sem, tok_s, tok_r, own_s, own_r, fwd_s, fwd_r, swap_s, swap_r, hgt_s, hgt_r, kvx_s, kvx_r,
):
    f, h, w = lax.axis_index("frame"), lax.axis_index("height"), lax.axis_index("width")
    f1 = f + 1 - 2 * (f % 2)
    f2 = f + 2 - 4 * ((f // 2) % 2)
    parity = f % 2
    side = w % 2
    rows = w_ref.shape[1]
    features = w_ref.shape[2]
    half = features // 2
    tokens = xn.shape[0] // 3
    frames = xs.shape[1]
    slots = kbuf.shape[0]
    heads = kbuf.shape[1] // 2
    group_rows = heads * HEAD_DIM
    local = n_h * rows // HEAD_DIM
    chunk = tokens // 2

    def place(owner_parity, group, row_parity, height):
        base = (owner_parity if group == 0 else 1 - owner_parity) * group_rows
        return pl.ds(pl.multiple_of(base + (row_parity * n_h + height) * rows, rows), rows)

    mine = place(parity, 0, parity, h)
    beside = place(parity, 0, 1 - parity, h)
    across = place(parity, 1, parity, h)
    corner = place(parity, 1, 1 - parity, h)

    def cols(s, p):
        at = p
        if s == QUERY:
            at = side if p == 0 else 1 - side
        return pl.ds(pl.multiple_of(at * half, half), half)

    def remote(src, dst, send, recv, target):
        return pltpu.make_async_remote_copy(
            src_ref=src, dst_ref=dst, send_sem=send, recv_sem=recv,
            device_id=target, device_id_type=MESH,
        )

    def to_frame(i):
        return ((f1, f2)[i], h, w)

    def own_copy(s, p, i):
        there = place(1 - parity, 0, parity, h) if i == 0 else across
        return remote(
            w_ref.at[s, :, cols(s, p)], w_all.at[s, there, cols(s, p)],
            own_s.at[s, p, i], own_r.at[s, p, i], to_frame(i),
        )

    def fwd_copy(s, i):
        if i == 1:
            src, there, at = beside, corner, cols(s, 0)
        else:
            src, there, at = across, place(1 - parity, 1, parity, h), cols(s, 1)
        return remote(w_all.at[s, src, at], w_all.at[s, there, at], fwd_s.at[s, i], fwd_r.at[s, i], to_frame(i))

    def swap_copy(i):
        part = w_all.at[QUERY, (beside, across)[i], cols(QUERY, i)]
        return remote(part, part, swap_s.at[i], swap_r.at[i], (f, h, w + 1 - 2 * side))

    def hgt_copy(s, piece, d):
        if piece == 0:
            src, dst = w_ref.at[s], w_all.at[s, mine]
        elif piece == 3:
            src = dst = w_all.at[s, corner]
        elif s != QUERY:
            src = dst = w_all.at[s, (beside, across)[piece - 1]]
        else:
            i = (piece - 1) % 3
            at = cols(s, i if piece < 3 else 1 - i)
            src = dst = w_all.at[s, (beside, across)[i], at]
        target = (f, lax.rem(h + d, n_h), w)
        return remote(src, dst, hgt_s.at[s, piece, d - 1], hgt_r.at[s, piece, d - 1], target)

    head_own = (parity * (2 * heads - local), local)
    head_beside = (local + parity * (heads - local), heads - local)
    head_across = (heads - parity * local, local)
    head_early = (parity * (heads - local), heads + local)
    head_late = ((1 - parity) * (heads + local), heads - local)

    kv_parts = (
        (head_early, 0, 2 * tokens),
        (head_early, 2 * tokens, tokens),
        (head_late, 0, 3 * tokens),
    )

    def kv_copy(which, part, up):
        buf = (kbuf, vbuf)[which]
        (first, count), start, length = kv_parts[part]
        slot = 1 if up or n_h == 2 else 2
        target = (f, h + 1 if up else h - 1, w)
        e = 0 if up else 1
        at = (pl.ds(first, count), pl.ds(start, length))
        return remote(
            buf.at[(0,) + at], buf.at[(slot,) + at], kvx_s.at[which, part, e], kvx_r.at[which, part, e], target
        )

    def tok_copy(e, c):
        target = (f, h, w + 1 if e == 0 else w - 1)
        at = pl.ds(c * (frames // 2), frames // 2)
        return remote(x_ref.at[0, at], xs.at[1 + e, at], tok_s.at[e, c], tok_r.at[e, c], target)

    local_x = pltpu.make_async_copy(x_ref.at[0], xs.at[0], loc_sem.at[0])
    local_w = [pltpu.make_async_copy(w_ref.at[s], w_all.at[s, mine], loc_sem.at[1 + s]) for s in range(3)]
    local_x.start()
    for s in (KEY, VALUE, QUERY):
        local_w[s].start()

    has_left, has_right = w > 0, w < n_w - 1
    has_below, has_above = h > 0, h < n_h - 1

    barrier = pltpu.get_barrier_semaphore()

    def greet(target):
        pl.semaphore_signal(barrier, inc=1, device_id=target, device_id_type=MESH)

    greet(to_frame(0))
    greet(to_frame(1))
    for d in range(1, n_h):
        greet((f, lax.rem(h + d, n_h), w))

    @pl.when(has_left)
    def _():
        greet((f, h, w - 1))

    @pl.when(has_right)
    def _():
        greet((f, h, w + 1))

    peers = n_h + 1 + has_left.astype(jnp.int32) + has_right.astype(jnp.int32)
    pl.semaphore_wait(barrier, peers)

    def send_own(s):
        own_copy(s, 0, 0).start()
        own_copy(s, 1, 1).start()
        if s != QUERY:
            own_copy(s, 1, 0).start()
            own_copy(s, 0, 1).start()

    def wait_own(s):
        own_copy(s, 0, 0).wait_recv()
        own_copy(s, 1, 1).wait_recv()
        fwd_copy(s, 0).start()
        fwd_copy(s, 1).start()
        if s == QUERY:
            swap_copy(0).start()
            swap_copy(1).start()
        else:
            own_copy(s, 1, 0).wait_recv()
            own_copy(s, 0, 1).wait_recv()
        relay(s, 1, 2)

    def relay(s, *pieces):
        for piece in pieces:
            for d in range(1, n_h):
                hgt_copy(s, piece, d).start()

    def take_fwd(s):
        fwd_copy(s, 0).wait_recv()
        fwd_copy(s, 1).wait_recv()
        relay(s, 3)

    def take_swap(i):
        swap_copy(i).wait_recv()
        relay(QUERY, 4 + i)

    def wait_hgt(s, *pieces):
        for piece in pieces:
            for d in range(1, n_h):
                hgt_copy(s, piece, d).wait_recv()

    for s in (KEY, VALUE, QUERY):
        send_own(s)
    for c in range(2):
        @pl.when(has_right)
        def _():
            tok_copy(0, c).start()

        @pl.when(has_left)
        def _():
            tok_copy(1, c).start()

    for s in (KEY, VALUE, QUERY):
        relay(s, 0)

    total_h, total_w = tm_ref.shape[2], tm_ref.shape[3]
    for b in range(slots):
        if b == 0:
            row_h = h
        elif n_h == 2:
            row_h = 1 - h
        else:
            row_h = h - 1 if b == 1 else h + 1

        def allow(c, first, count, start):
            shape = (tokens, count * CUBE)
            q_tile = lax.broadcasted_iota(jnp.int32, shape, 0) // CUBE
            k_tile = lax.broadcasted_iota(jnp.int32, shape, 1) // CUBE + first
            col_w = w + (0, -1, 1)[c]
            inside = ((row_h >= 0) & (row_h < total_h) & (col_w >= 0) & (col_w < total_w)).astype(jnp.int32)
            at_h = jnp.minimum(jnp.maximum(row_h, 0), total_h - 1)
            at_w = jnp.minimum(jnp.maximum(col_w, 0), total_w - 1)
            flags = jnp.zeros(shape, jnp.int32)
            for t in range(first, first + count):
                flag = tm_ref[0, t, at_h, at_w] * inside
                flags = jnp.where(k_tile == t, flag, flags)
            seen = flags == 1
            if b == 0 and c == 0:
                seen = seen | (q_tile == k_tile)
            allowed = jnp.where((jnp.abs(q_tile - k_tile) <= 1) & seen, jnp.float32(1.0), jnp.float32(0.0))
            mask[b, :, start : start + count * CUBE] = allowed.astype(jnp.bfloat16)

        allow(0, 0, tokens // CUBE, 0)
        for c in range(2):
            for e in range(2):
                allow(1 + e, c * (chunk // CUBE), chunk // CUBE, tokens + (2 * c + e) * chunk)

    step = 64

    def normalise(c, frame, start, count):
        for t in range(count // step):
            each = step // (TILE * TILE)
            block = xs[c, frame + t * each : frame + (t + 1) * each].astype(jnp.float32).reshape(step, features)
            scale = lax.rsqrt(jnp.mean(block * block, -1, keepdims=True) + epsilon)
            xn[start + t * step : start + (t + 1) * step, :] = (block * scale).astype(jnp.bfloat16)

    def take_tokens(c):
        for e, here in ((0, has_left), (1, has_right)):
            start = tokens + (2 * c + e) * chunk

            @pl.when(here)
            def _():
                tok_copy(e, c).wait_recv()
                normalise(1 + e, c * (frames // 2), start, chunk)

            @pl.when(jnp.logical_not(here))
            def _():
                xn[start : start + chunk, :] = jnp.zeros((chunk, features), jnp.bfloat16)

    def head_norm(raw):
        return (raw * lax.rsqrt(jnp.mean(raw * raw, -1, keepdims=True) + epsilon)).astype(jnp.bfloat16)

    contract_last = (((1,), (1,)), ((), ()))

    def project(s, some, start, length):
        first, count = some
        place_rows = pl.ds(pl.multiple_of(first * HEAD_DIM, HEAD_DIM), count * HEAD_DIM)
        raw = lax.dot_general(
            xn[start : start + length, :], w_all[s, place_rows], contract_last, preferred_element_type=jnp.float32
        )
        for j in range(count):
            part = raw[:, j * HEAD_DIM : (j + 1) * HEAD_DIM]
            if s == QUERY:
                qbuf[first + j] = head_norm(part)
            elif s == KEY:
                kbuf[0, first + j, start : start + length, :] = head_norm(part)
            else:
                vbuf[0, first + j, start : start + length, :] = part.astype(jnp.bfloat16)

    def send_kv(which, part):
        @pl.when(has_above)
        def _():
            kv_copy(which, part, True).start()

        @pl.when(has_below)
        def _():
            kv_copy(which, part, False).start()

    def wait_kv(*parts):
        for part in parts:
            for which in range(2):
                @pl.when(has_below)
                def _():
                    kv_copy(which, part, True).wait_recv()

                @pl.when(has_above)
                def _():
                    kv_copy(which, part, False).wait_recv()

    factor = HEAD_DIM ** (-0.5) * math.log2(math.e)
    ones = jnp.ones((3 * tokens, HEAD_DIM), jnp.bfloat16)
    pair = f // 2

    def attend(some):
        first, count = some

        def body(i, carry):
            j = first + i
            q = qbuf[j]
            total = jnp.zeros((tokens, 2 * HEAD_DIM), jnp.float32)
            for b in range(slots):
                scores = lax.dot_general(q, kbuf[b, j], contract_last, preferred_element_type=jnp.float32)
                weight = jnp.exp2(scores * factor).astype(jnp.bfloat16) * mask[b]
                wide = jnp.concatenate([vbuf[b, j], ones], 1)
                total = total + jnp.dot(weight, wide, preferred_element_type=jnp.float32)
            result = (total[:, :HEAD_DIM] / total[:, HEAD_DIM:]).astype(o_ref.dtype)
            upper = (j >= heads).astype(jnp.int32)
            group = lax.rem(pair + parity + upper, 2)
            at = (group * heads + j - upper * heads) * HEAD_DIM
            o_ref[:, pl.ds(pl.multiple_of(at, HEAD_DIM), HEAD_DIM)] = result
            return carry

        lax.fori_loop(0, count, body, 0)

    if n_h > 2:
        for edge, slot in ((h == 0, 1), (h == n_h - 1, 2)):
            @pl.when(edge)
            def _():
                kbuf[slot] = jnp.zeros(kbuf.shape[1:], jnp.bfloat16)
                vbuf[slot] = jnp.zeros(vbuf.shape[1:], jnp.bfloat16)

    local_x.wait()
    normalise(0, 0, 0, tokens)
    wait_own(KEY)
    take_tokens(0)
    local_w[KEY].wait()
    wait_hgt(KEY, 0, 1, 2)
    project(KEY, head_early, 0, 2 * tokens)
    send_kv(0, 0)
    wait_own(VALUE)
    local_w[VALUE].wait()
    wait_hgt(VALUE, 0, 1, 2)
    project(VALUE, head_early, 0, 2 * tokens)
    send_kv(1, 0)
    local_w[QUERY].wait()
    wait_hgt(QUERY, 0)
    project(QUERY, head_own, 0, tokens)
    wait_own(QUERY)
    take_tokens(1)
    project(KEY, head_early, 2 * tokens, tokens)
    send_kv(0, 1)
    project(VALUE, head_early, 2 * tokens, tokens)
    send_kv(1, 1)
    take_fwd(KEY)
    wait_kv(0, 1)
    attend(head_own)
    wait_hgt(KEY, 3)
    project(KEY, head_late, 0, 3 * tokens)
    send_kv(0, 2)
    take_swap(0)
    take_fwd(VALUE)
    wait_hgt(QUERY, 1, 4)
    project(QUERY, head_beside, 0, tokens)
    wait_hgt(VALUE, 3)
    project(VALUE, head_late, 0, 3 * tokens)
    send_kv(1, 2)
    attend(head_beside)
    take_swap(1)
    take_fwd(QUERY)
    wait_hgt(QUERY, 2, 5)
    project(QUERY, head_across, 0, tokens)
    attend(head_across)
    wait_kv(2)
    wait_hgt(QUERY, 3)
    project(QUERY, head_late, 0, tokens)
    attend(head_late)

    for s in range(3):
        for i in range(2):
            own_copy(s, i, i).wait_send()
            fwd_copy(s, i).wait_send()
            if s != QUERY:
                own_copy(s, 1 - i, i).wait_send()
        for piece in range(6 if s == QUERY else 4):
            for d in range(1, n_h):
                hgt_copy(s, piece, d).wait_send()
    for i in range(2):
        swap_copy(i).wait_send()

    for c in range(2):
        @pl.when(has_right)
        def _():
            tok_copy(0, c).wait_send()

        @pl.when(has_left)
        def _():
            tok_copy(1, c).wait_send()

    for part in range(3):
        for which in range(2):
            @pl.when(has_above)
            def _():
                kv_copy(which, part, True).wait_send()

            @pl.when(has_below)
            def _():
                kv_copy(which, part, False).wait_send()


def per_device(n_f, n_h, n_w, tokens, qkv_weight, tile_mask):
    clips, frames, rows, columns, features = tokens.shape
    count = frames * rows * columns
    width = qkv_weight.shape[1] * n_f * n_h
    if n_f != 4 or n_h < 2 or n_w % 2 or clips != 1 or rows != TILE or columns != TILE:
        raise ValueError("unsupported placement")
    heads = width // HEAD_DIM
    slots = 2 if n_h == 2 else 3
    dma = pltpu.SemaphoreType.DMA
    out = pl.pallas_call(
        functools.partial(kernel, n_h, n_w),
        out_shape=jax.ShapeDtypeStruct((count, width), jnp.bfloat16),
        in_specs=[
            pl.BlockSpec(memory_space=pl.ANY),
            pl.BlockSpec(memory_space=pl.ANY),
            pl.BlockSpec(memory_space=pltpu.SMEM),
        ],
        out_specs=pl.BlockSpec(memory_space=pltpu.VMEM),
        scratch_shapes=[
            pltpu.VMEM((3, frames, rows, columns, features), jnp.bfloat16),
            pltpu.VMEM((3 * count, features), jnp.bfloat16),
            pltpu.VMEM((3, width, features), jnp.bfloat16),
            pltpu.VMEM((slots, heads, 3 * count, HEAD_DIM), jnp.bfloat16),
            pltpu.VMEM((slots, heads, 3 * count, HEAD_DIM), jnp.bfloat16),
            pltpu.VMEM((heads, count, HEAD_DIM), jnp.bfloat16),
            pltpu.VMEM((slots, count, 3 * count), jnp.bfloat16),
            dma((4,)), dma((2, 2)), dma((2, 2)), dma((3, 2, 2)), dma((3, 2, 2)), dma((3, 2)), dma((3, 2)),
            dma((2,)), dma((2,)), dma((3, 6, n_h - 1)), dma((3, 6, n_h - 1)), dma((2, 3, 2)), dma((2, 3, 2)),
        ],
        compiler_params=pltpu.CompilerParams(
            collective_id=0, has_side_effects=True, vmem_limit_bytes=VMEM_LIMIT
        ),
    )(tokens, qkv_weight, tile_mask)
    return out.reshape(clips, frames, rows, columns, width)


def solution(mesh):
    in_specs = (
        P("frame", None, "height", "width", None),
        P(None, ("frame", "height"), None),
        P("frame", None, None, None),
    )
    out_specs = P("frame", None, "height", "width", None)
    body = functools.partial(
        per_device, mesh.shape["frame"], mesh.shape["height"], mesh.shape["width"]
    )
    return jax.shard_map(body, mesh=mesh, in_specs=in_specs, out_specs=out_specs, check_vma=False)
```

time: 45.8 us -> 41.5 us (0.906)
  Pallas kernels: 43.8 us -> 39.8 us
    pallas_call x1, Pallas kernels: 43.8 us -> 39.8 us  [per_device(): pl.pallas_call(functools.partial(kernel, n_h, n_w), out_shape=jax.ShapeDt...]
    reshape x1, local copies, waits for them, and re-layouts: 1.84 us -> 0.84 us  [per_device(): return out.reshape(clips, frames, rows, columns, width)]
    unnamed x0 -> x2, local copies, waits for them, and re-layouts: none -> 0.69 us
where the time goes in v1:
time: 41.5 us; the launch traced here: 41.3 us
  Pallas kernels  39.8 us (96%)
  local copies, waits for them, and re-layouts  1.53 us (4%)
    pallas_call x1, Pallas kernels, per_device(): pl.pallas_call(functools.partial(kernel, n_h, n_w), out_shape=jax.ShapeDt...  39.8 us
    reshape x1, local copies, waits for them, and re-layouts, per_device(): return out.reshape(clips, frames, rows, columns, width)  0.84 us

profile of v1, /device:TPU:0, one launch (start us, length us, event | category | flops | bytes accessed | tf_op | source)
XLA Modules:
  0.0 41.3 jit_solution(1889307205897852821)
XLA Ops:
  0.0 0.0 copy-start
  0.0 0.7 %copy-done = s32[1,4,2,4]{3,2,1,0:T(2,128)S(1)} copy-done((s32[1,4,2,4]{3,2,1,0:T(2,128)S(1)}, s32[1,4,2,4]{3,2,1,0:T(2,128)}, u32[]{:S(2)}) %copy-start) | copy-done | bytes 152
  0.7 39.8 %shard_map.37 = bf16[256,768]{1,0:T(8,128)(2,1)S(1)} custom-call(bf16[1,16,4,4,1536]{4,3,2,1,0:T(4,128)(2,1)} %x_ref.1, bf16[3,96,1536]{2,1,0:T(8,128)(2,1)} %w_ref.1, s32[1,4,2,4]{3,2,1,0:T(2,128)S(1)} %copy-done), custom_call_target="tpu_custom_call" | custom-call | tf_op jit(solution)/shard_map/pallas_call | solution.py:422
  40.5 0.8 %reshape.3 = bf16[1,16,4,4,768]{4,3,2,1,0:T(4,128)(2,1)} reshape(bf16[256,768]{1,0:T(8,128)(2,1)S(1)} %shard_map.37) | data formatting | bytes 786432 | tf_op jit(solution)/shard_map/reshape | solution.py:446
Async XLA Ops:
  0.0 0.7 %copy-start = (s32[1,4,2,4]{3,2,1,0:T(2,128)S(1)}, s32[1,4,2,4]{3,2,1,0:T(2,128)}, u32[]{:S(2)}) copy-start(s32[1,4,2,4]{3,2,1,0:T(2,128)} %tm_ref.1) | copy-start | bytes 388

commit v2 on v1

--- a/solution.py
+++ b/solution.py
@@ -32,9 +32,10 @@
     features = w_ref.shape[2]
     half = features // 2
     tokens = xn.shape[0] // 3
+    span = 3 * tokens
+    slots = kbuf.shape[1] // span
     frames = xs.shape[1]
-    slots = kbuf.shape[0]
-    heads = kbuf.shape[1] // 2
+    heads = kbuf.shape[0] // 2
     group_rows = heads * HEAD_DIM
     local = n_h * rows // HEAD_DIM
     chunk = tokens // 2
@@ -97,7 +98,7 @@
 
     head_own = (parity * (2 * heads - local), local)
     head_beside = (local + parity * (heads - local), heads - local)
-    head_across = (heads - parity * local, local)
+    head_other = ((1 - parity) * heads, heads)
     head_early = (parity * (heads - local), heads + local)
     head_late = ((1 - parity) * (heads + local), heads - local)
 
@@ -113,10 +114,10 @@
         slot = 1 if up or n_h == 2 else 2
         target = (f, h + 1 if up else h - 1, w)
         e = 0 if up else 1
-        at = (pl.ds(first, count), pl.ds(start, length))
-        return remote(
-            buf.at[(0,) + at], buf.at[(slot,) + at], kvx_s.at[which, part, e], kvx_r.at[which, part, e], target
-        )
+        some = pl.ds(first, count)
+        src = buf.at[some, pl.ds(start, length)]
+        dst = buf.at[some, pl.ds(slot * span + start, length)]
+        return remote(src, dst, kvx_s.at[which, part, e], kvx_r.at[which, part, e], target)
 
     def tok_copy(e, c):
         target = (f, h, w + 1 if e == 0 else w - 1)
@@ -231,7 +232,8 @@
             if b == 0 and c == 0:
                 seen = seen | (q_tile == k_tile)
             allowed = jnp.where((jnp.abs(q_tile - k_tile) <= 1) & seen, jnp.float32(1.0), jnp.float32(0.0))
-            mask[b, :, start : start + count * CUBE] = allowed.astype(jnp.bfloat16)
+            start = b * span + start
+            mask[:, start : start + count * CUBE] = allowed.astype(jnp.bfloat16)
 
         allow(0, 0, tokens // CUBE, 0)
         for c in range(2):
@@ -276,9 +278,9 @@
             if s == QUERY:
                 qbuf[first + j] = head_norm(part)
             elif s == KEY:
-                kbuf[0, first + j, start : start + length, :] = head_norm(part)
+                kbuf[first + j, start : start + length, :] = head_norm(part)
             else:
-                vbuf[0, first + j, start : start + length, :] = part.astype(jnp.bfloat16)
+                vbuf[first + j, start : start + length, :] = part.astype(jnp.bfloat16)
 
     def send_kv(which, part):
         @pl.when(has_above)
@@ -301,36 +303,31 @@
                     kv_copy(which, part, False).wait_recv()
 
     factor = HEAD_DIM ** (-0.5) * math.log2(math.e)
-    ones = jnp.ones((3 * tokens, HEAD_DIM), jnp.bfloat16)
+    ones = jnp.ones((slots * span, HEAD_DIM), jnp.bfloat16)
     pair = f // 2
 
     def attend(some):
         first, count = some
 
-        def body(i, carry):
+        for i in range(count):
             j = first + i
-            q = qbuf[j]
-            total = jnp.zeros((tokens, 2 * HEAD_DIM), jnp.float32)
-            for b in range(slots):
-                scores = lax.dot_general(q, kbuf[b, j], contract_last, preferred_element_type=jnp.float32)
-                weight = jnp.exp2(scores * factor).astype(jnp.bfloat16) * mask[b]
-                wide = jnp.concatenate([vbuf[b, j], ones], 1)
-                total = total + jnp.dot(weight, wide, preferred_element_type=jnp.float32)
+            scores = lax.dot_general(qbuf[j], kbuf[j], contract_last, preferred_element_type=jnp.float32)
+            weight = jnp.exp2(scores * factor).astype(jnp.bfloat16) * mask[...]
+            wide = jnp.concatenate([vbuf[j], ones], 1)
+            total = jnp.dot(weight, wide, preferred_element_type=jnp.float32)
             result = (total[:, :HEAD_DIM] / total[:, HEAD_DIM:]).astype(o_ref.dtype)
             upper = (j >= heads).astype(jnp.int32)
             group = lax.rem(pair + parity + upper, 2)
             at = (group * heads + j - upper * heads) * HEAD_DIM
             o_ref[:, pl.ds(pl.multiple_of(at, HEAD_DIM), HEAD_DIM)] = result
-            return carry
-
-        lax.fori_loop(0, count, body, 0)
 
     if n_h > 2:
         for edge, slot in ((h == 0, 1), (h == n_h - 1, 2)):
             @pl.when(edge)
             def _():
-                kbuf[slot] = jnp.zeros(kbuf.shape[1:], jnp.bfloat16)
-                vbuf[slot] = jnp.zeros(vbuf.shape[1:], jnp.bfloat16)
+                at = slice(slot * span, (slot + 1) * span)
+                kbuf[:, at] = jnp.zeros((2 * heads, span, HEAD_DIM), jnp.bfloat16)
+                vbuf[:, at] = jnp.zeros((2 * heads, span, HEAD_DIM), jnp.bfloat16)
 
     local_x.wait()
     normalise(0, 0, 0, tokens)
@@ -352,31 +349,29 @@
     take_tokens(1)
     project(KEY, head_early, 2 * tokens, tokens)
     send_kv(0, 1)
+    take_fwd(KEY)
     project(VALUE, head_early, 2 * tokens, tokens)
     send_kv(1, 1)
-    take_fwd(KEY)
-    wait_kv(0, 1)
-    attend(head_own)
     wait_hgt(KEY, 3)
     project(KEY, head_late, 0, 3 * tokens)
     send_kv(0, 2)
     take_swap(0)
     take_fwd(VALUE)
-    wait_hgt(QUERY, 1, 4)
-    project(QUERY, head_beside, 0, tokens)
+    wait_kv(0, 1)
+    attend(head_own)
     wait_hgt(VALUE, 3)
     project(VALUE, head_late, 0, 3 * tokens)
     send_kv(1, 2)
-    attend(head_beside)
+    wait_hgt(QUERY, 1, 4)
+    project(QUERY, head_beside, 0, tokens)
     take_swap(1)
+    attend((head_beside[0], 1))
     take_fwd(QUERY)
-    wait_hgt(QUERY, 2, 5)
-    project(QUERY, head_across, 0, tokens)
-    attend(head_across)
+    attend((head_beside[0] + 1, head_beside[1] - 1))
+    wait_hgt(QUERY, 2, 5, 3)
+    project(QUERY, head_other, 0, tokens)
     wait_kv(2)
-    wait_hgt(QUERY, 3)
-    project(QUERY, head_late, 0, tokens)
-    attend(head_late)
+    attend(head_other)
 
     for s in range(3):
         for i in range(2):
@@ -423,8 +418,8 @@
         functools.partial(kernel, n_h, n_w),
         out_shape=jax.ShapeDtypeStruct((count, width), jnp.bfloat16),
         in_specs=[
-            pl.BlockSpec(memory_space=pl.ANY),
-            pl.BlockSpec(memory_space=pl.ANY),
+            pl.BlockSpec(memory_space=pltpu.HBM),
+            pl.BlockSpec(memory_space=pltpu.HBM),
             pl.BlockSpec(memory_space=pltpu.SMEM),
         ],
         out_specs=pl.BlockSpec(memory_space=pltpu.VMEM),
@@ -432,17 +427,17 @@
             pltpu.VMEM((3, frames, rows, columns, features), jnp.bfloat16),
             pltpu.VMEM((3 * count, features), jnp.bfloat16),
             pltpu.VMEM((3, width, features), jnp.bfloat16),
-            pltpu.VMEM((slots, heads, 3 * count, HEAD_DIM), jnp.bfloat16),
-            pltpu.VMEM((slots, heads, 3 * count, HEAD_DIM), jnp.bfloat16),
+            pltpu.VMEM((heads, slots * 3 * count, HEAD_DIM), jnp.bfloat16),
+            pltpu.VMEM((heads, slots * 3 * count, HEAD_DIM), jnp.bfloat16),
             pltpu.VMEM((heads, count, HEAD_DIM), jnp.bfloat16),
-            pltpu.VMEM((slots, count, 3 * count), jnp.bfloat16),
+            pltpu.VMEM((count, slots * 3 * count), jnp.bfloat16),
             dma((4,)), dma((2, 2)), dma((2, 2)), dma((3, 2, 2)), dma((3, 2, 2)), dma((3, 2)), dma((3, 2)),
             dma((2,)), dma((2,)), dma((3, 6, n_h - 1)), dma((3, 6, n_h - 1)), dma((2, 3, 2)), dma((2, 3, 2)),
         ],
         compiler_params=pltpu.CompilerParams(
             collective_id=0, has_side_effects=True, vmem_limit_bytes=VMEM_LIMIT
         ),
-    )(tokens, qkv_weight, tile_mask)
+    )(*(pltpu.with_memory_space_constraint(a, pltpu.HBM) for a in (tokens, qkv_weight, tile_mask)))
     return out.reshape(clips, frames, rows, columns, width)
 
 

time: 41.5 us -> 39.2 us (0.945)
  Pallas kernels: 39.8 us -> 38.2 us
  local copies, waits for them, and re-layouts: 1.53 us -> 0.84 us
    pallas_call x1, Pallas kernels: 39.8 us -> 38.2 us  [per_device(): pl.pallas_call(functools.partial(kernel, n_h, n_w), out_shape=jax.ShapeDt...]
    unnamed x2 -> x0, local copies, waits for them, and re-layouts: 0.69 us -> none
where the time goes in v2:
time: 39.2 us; the launch traced here: 39 us
  Pallas kernels  38.2 us (97%)
  local copies, waits for them, and re-layouts  0.84 us (2%)
    pallas_call x1, Pallas kernels, per_device(): pl.pallas_call(functools.partial(kernel, n_h, n_w), out_shape=jax.ShapeDt...  38.2 us
    reshape x1, local copies, waits for them, and re-layouts, per_device(): return out.reshape(clips, frames, rows, columns, width)  0.84 us

profile of v2, /device:TPU:0, one launch (start us, length us, event | category | flops | bytes accessed | tf_op | source)
XLA Modules:
  0.0 39.0 jit_solution(6905275909149665091)
XLA Ops:
  0.0 38.2 %shard_map.37 = bf16[256,768]{1,0:T(8,128)(2,1)S(1)} custom-call(bf16[1,16,4,4,1536]{4,3,2,1,0:T(4,128)(2,1)} %x_ref.1, bf16[3,96,1536]{2,1,0:T(8,128)(2,1)} %w_ref.1, s32[1,4,2,4]{3,2,1,0:T(2,128)} %tm_ref.1), custom_call_target="tpu_custom_call" | custom-call | tf_op jit(solution)/shard_map/pallas_call | solution.py:417
  38.2 0.8 %reshape.3 = bf16[1,16,4,4,768]{4,3,2,1,0:T(4,128)(2,1)} reshape(bf16[256,768]{1,0:T(8,128)(2,1)S(1)} %shard_map.37) | data formatting | bytes 786432 | tf_op jit(solution)/shard_map/reshape | solution.py:441

commit v3 on v2

--- a/solution.py
+++ b/solution.py
@@ -20,7 +20,7 @@
 
 def kernel(
     n_h, n_w, x_ref, w_ref, tm_ref, o_ref,
-    xs, xn, w_all, kbuf, vbuf, qbuf, mask,
+    flags_ref, xs, xn, w_all, kbuf, vbuf, qbuf, mask,
     loc_sem, tok_s, tok_r, own_s, own_r, fwd_s, fwd_r, swap_s, swap_r, hgt_s, hgt_r, kvx_s, kvx_r,
 ):
     f, h, w = lax.axis_index("frame"), lax.axis_index("height"), lax.axis_index("width")
@@ -32,13 +32,18 @@
     features = w_ref.shape[2]
     half = features // 2
     tokens = xn.shape[0] // 3
-    span = 3 * tokens
-    slots = kbuf.shape[1] // span
-    frames = xs.shape[1]
+    span = 3 * CUBE
+    slots = kbuf.shape[2] // span
     heads = kbuf.shape[0] // 2
     group_rows = heads * HEAD_DIM
     local = n_h * rows // HEAD_DIM
-    chunk = tokens // 2
+    tiles = tokens // CUBE
+    halo = ((0, tiles - 1), (tiles - 1, 1))
+    early_tokens = tokens + 2 * halo[0][1] * CUBE
+    late_tokens = 2 * halo[1][1] * CUBE
+
+    def halo_start(c, e):
+        return (tokens, early_tokens)[c] + e * halo[c][1] * CUBE
 
     def place(owner_parity, group, row_parity, height):
         base = (owner_parity if group == 0 else 1 - owner_parity) * group_rows
@@ -102,11 +107,7 @@
     head_early = (parity * (heads - local), heads + local)
     head_late = ((1 - parity) * (heads + local), heads - local)
 
-    kv_parts = (
-        (head_early, 0, 2 * tokens),
-        (head_early, 2 * tokens, tokens),
-        (head_late, 0, 3 * tokens),
-    )
+    kv_parts = ((head_early, *halo[0]), (head_early, *halo[1]), (head_late, 0, tiles))
 
     def kv_copy(which, part, up):
         buf = (kbuf, vbuf)[which]
@@ -114,22 +115,19 @@
         slot = 1 if up or n_h == 2 else 2
         target = (f, h + 1 if up else h - 1, w)
         e = 0 if up else 1
-        some = pl.ds(first, count)
-        src = buf.at[some, pl.ds(start, length)]
-        dst = buf.at[some, pl.ds(slot * span + start, length)]
+        some = (pl.ds(first, count), pl.ds(start, length))
+        src = buf.at[some + (pl.ds(0, span),)]
+        dst = buf.at[some + (pl.ds(slot * span, span),)]
         return remote(src, dst, kvx_s.at[which, part, e], kvx_r.at[which, part, e], target)
 
     def tok_copy(e, c):
         target = (f, h, w + 1 if e == 0 else w - 1)
-        at = pl.ds(c * (frames // 2), frames // 2)
+        at = pl.ds(halo[c][0] * TILE, halo[c][1] * TILE)
         return remote(x_ref.at[0, at], xs.at[1 + e, at], tok_s.at[e, c], tok_r.at[e, c], target)
 
+    local_mask = pltpu.make_async_copy(tm_ref, flags_ref, loc_sem.at[4])
     local_x = pltpu.make_async_copy(x_ref.at[0], xs.at[0], loc_sem.at[0])
     local_w = [pltpu.make_async_copy(w_ref.at[s], w_all.at[s, mine], loc_sem.at[1 + s]) for s in range(3)]
-    local_x.start()
-    for s in (KEY, VALUE, QUERY):
-        local_w[s].start()
-
     has_left, has_right = w > 0, w < n_w - 1
     has_below, has_above = h > 0, h < n_h - 1
 
@@ -152,6 +150,10 @@
         greet((f, h, w + 1))
 
     peers = n_h + 1 + has_left.astype(jnp.int32) + has_right.astype(jnp.int32)
+    local_mask.start()
+    local_x.start()
+    for s in (KEY, VALUE, QUERY):
+        local_w[s].start()
     pl.semaphore_wait(barrier, peers)
 
     def send_own(s):
@@ -207,38 +209,32 @@
     for s in (KEY, VALUE, QUERY):
         relay(s, 0)
 
+    local_mask.wait()
     total_h, total_w = tm_ref.shape[2], tm_ref.shape[3]
-    for b in range(slots):
-        if b == 0:
-            row_h = h
-        elif n_h == 2:
-            row_h = 1 - h
-        else:
-            row_h = h - 1 if b == 1 else h + 1
-
-        def allow(c, first, count, start):
-            shape = (tokens, count * CUBE)
-            q_tile = lax.broadcasted_iota(jnp.int32, shape, 0) // CUBE
-            k_tile = lax.broadcasted_iota(jnp.int32, shape, 1) // CUBE + first
-            col_w = w + (0, -1, 1)[c]
-            inside = ((row_h >= 0) & (row_h < total_h) & (col_w >= 0) & (col_w < total_w)).astype(jnp.int32)
-            at_h = jnp.minimum(jnp.maximum(row_h, 0), total_h - 1)
-            at_w = jnp.minimum(jnp.maximum(col_w, 0), total_w - 1)
-            flags = jnp.zeros(shape, jnp.int32)
-            for t in range(first, first + count):
-                flag = tm_ref[0, t, at_h, at_w] * inside
-                flags = jnp.where(k_tile == t, flag, flags)
-            seen = flags == 1
-            if b == 0 and c == 0:
-                seen = seen | (q_tile == k_tile)
-            allowed = jnp.where((jnp.abs(q_tile - k_tile) <= 1) & seen, jnp.float32(1.0), jnp.float32(0.0))
-            start = b * span + start
-            mask[:, start : start + count * CUBE] = allowed.astype(jnp.bfloat16)
-
-        allow(0, 0, tokens // CUBE, 0)
-        for c in range(2):
-            for e in range(2):
-                allow(1 + e, c * (chunk // CUBE), chunk // CUBE, tokens + (2 * c + e) * chunk)
+    shape = (tokens, slots * span)
+    q_tile = lax.broadcasted_iota(jnp.int32, shape, 0) // CUBE
+    block = lax.broadcasted_iota(jnp.int32, shape, 1) // CUBE
+    for t in range(tiles):
+        seen = jnp.zeros(shape, jnp.int32)
+        for b in range(slots):
+            if b == 0:
+                row_h = h
+            elif n_h == 2:
+                row_h = 1 - h
+            else:
+                row_h = h - 1 if b == 1 else h + 1
+            for c in range(3):
+                col_w = w + (0, -1, 1)[c]
+                inside = ((row_h >= 0) & (row_h < total_h) & (col_w >= 0) & (col_w < total_w)).astype(jnp.int32)
+                at_h = jnp.minimum(jnp.maximum(row_h, 0), total_h - 1)
+                at_w = jnp.minimum(jnp.maximum(col_w, 0), total_w - 1)
+                flag = flags_ref[0, t, at_h, at_w] * inside
+                seen = jnp.where(block == 3 * b + c, flag, seen)
+        near = jnp.abs(q_tile - t) <= 1
+        allowed = near & ((seen == 1) | ((block == 0) & (q_tile == t)))
+        mask[:, t * slots * span : (t + 1) * slots * span] = jnp.where(
+            allowed, jnp.float32(1.0), jnp.float32(0.0)
+        ).astype(jnp.bfloat16)
 
     step = 64
 
@@ -251,12 +247,12 @@
 
     def take_tokens(c):
         for e, here in ((0, has_left), (1, has_right)):
-            start = tokens + (2 * c + e) * chunk
+            start, chunk = halo_start(c, e), halo[c][1] * CUBE
 
             @pl.when(here)
             def _():
                 tok_copy(e, c).wait_recv()
-                normalise(1 + e, c * (frames // 2), start, chunk)
+                normalise(1 + e, halo[c][0] * TILE, start, chunk)
 
             @pl.when(jnp.logical_not(here))
             def _():
@@ -266,6 +262,11 @@
         return (raw * lax.rsqrt(jnp.mean(raw * raw, -1, keepdims=True) + epsilon)).astype(jnp.bfloat16)
 
     contract_last = (((1,), (1,)), ((), ()))
+
+    blocks = [(t, 0, t * CUBE) for t in range(tiles)]
+    for c in range(2):
+        for e in range(2):
+            blocks += [(halo[c][0] + t, 1 + e, halo_start(c, e) + t * CUBE) for t in range(halo[c][1])]
 
     def project(s, some, start, length):
         first, count = some
@@ -277,10 +278,12 @@
             part = raw[:, j * HEAD_DIM : (j + 1) * HEAD_DIM]
             if s == QUERY:
                 qbuf[first + j] = head_norm(part)
-            elif s == KEY:
-                kbuf[first + j, start : start + length, :] = head_norm(part)
-            else:
-                vbuf[first + j, start : start + length, :] = part.astype(jnp.bfloat16)
+                continue
+            buf = kbuf if s == KEY else vbuf
+            part = head_norm(part) if s == KEY else part.astype(jnp.bfloat16)
+            for t, c, at in blocks:
+                if start <= at < start + length:
+                    buf[first + j, t, c * CUBE : (c + 1) * CUBE, :] = part[at - start : at - start + CUBE]
 
     def send_kv(which, part):
         @pl.when(has_above)
@@ -303,7 +306,6 @@
                     kv_copy(which, part, False).wait_recv()
 
     factor = HEAD_DIM ** (-0.5) * math.log2(math.e)
-    ones = jnp.ones((slots * span, HEAD_DIM), jnp.bfloat16)
     pair = f // 2
 
     def attend(some):
@@ -311,62 +313,70 @@
 
         for i in range(count):
             j = first + i
-            scores = lax.dot_general(qbuf[j], kbuf[j], contract_last, preferred_element_type=jnp.float32)
-            weight = jnp.exp2(scores * factor).astype(jnp.bfloat16) * mask[...]
-            wide = jnp.concatenate([vbuf[j], ones], 1)
-            total = jnp.dot(weight, wide, preferred_element_type=jnp.float32)
-            result = (total[:, :HEAD_DIM] / total[:, HEAD_DIM:]).astype(o_ref.dtype)
+            keys = kbuf[j].reshape(tiles * slots * span, HEAD_DIM)
+            values = vbuf[j].reshape(tiles * slots * span, HEAD_DIM)
+            scores = lax.dot_general(qbuf[j], keys, contract_last, preferred_element_type=jnp.float32)
             upper = (j >= heads).astype(jnp.int32)
             group = lax.rem(pair + parity + upper, 2)
             at = (group * heads + j - upper * heads) * HEAD_DIM
-            o_ref[:, pl.ds(pl.multiple_of(at, HEAD_DIM), HEAD_DIM)] = result
+            lanes = pl.ds(pl.multiple_of(at, HEAD_DIM), HEAD_DIM)
+            for t in range(0, tiles, 2):
+                queries = slice(t * CUBE, min(t + 2, tiles) * CUBE)
+                near = slice(max(t - 1, 0) * slots * span, min(t + 3, tiles) * slots * span)
+                weight = jnp.exp2(scores[queries, near] * factor).astype(jnp.bfloat16) * mask[queries, near]
+                ones = jnp.ones((near.stop - near.start, HEAD_DIM), jnp.bfloat16)
+                wide = jnp.concatenate([values[near], ones], 1)
+                total = jnp.dot(weight, wide, preferred_element_type=jnp.float32)
+                o_ref[queries, lanes] = (total[:, :HEAD_DIM] / total[:, HEAD_DIM:]).astype(o_ref.dtype)
 
     if n_h > 2:
         for edge, slot in ((h == 0, 1), (h == n_h - 1, 2)):
             @pl.when(edge)
             def _():
                 at = slice(slot * span, (slot + 1) * span)
-                kbuf[:, at] = jnp.zeros((2 * heads, span, HEAD_DIM), jnp.bfloat16)
-                vbuf[:, at] = jnp.zeros((2 * heads, span, HEAD_DIM), jnp.bfloat16)
+                blank = jnp.zeros((2 * heads, tiles, span, HEAD_DIM), jnp.bfloat16)
+                kbuf[:, :, at] = blank
+                vbuf[:, :, at] = blank
 
     local_x.wait()
     normalise(0, 0, 0, tokens)
     wait_own(KEY)
-    take_tokens(0)
     local_w[KEY].wait()
     wait_hgt(KEY, 0, 1, 2)
-    project(KEY, head_early, 0, 2 * tokens)
+    project(KEY, head_early, 0, tokens)
+    wait_own(VALUE)
+    take_tokens(0)
+    project(KEY, head_early, tokens, early_tokens - tokens)
     send_kv(0, 0)
-    wait_own(VALUE)
     local_w[VALUE].wait()
     wait_hgt(VALUE, 0, 1, 2)
-    project(VALUE, head_early, 0, 2 * tokens)
+    project(VALUE, head_early, 0, early_tokens)
     send_kv(1, 0)
     local_w[QUERY].wait()
     wait_hgt(QUERY, 0)
     project(QUERY, head_own, 0, tokens)
     wait_own(QUERY)
     take_tokens(1)
-    project(KEY, head_early, 2 * tokens, tokens)
+    project(KEY, head_early, early_tokens, late_tokens)
     send_kv(0, 1)
+    project(VALUE, head_early, early_tokens, late_tokens)
+    send_kv(1, 1)
     take_fwd(KEY)
-    project(VALUE, head_early, 2 * tokens, tokens)
-    send_kv(1, 1)
+    wait_kv(0, 1)
+    attend(head_own)
     wait_hgt(KEY, 3)
     project(KEY, head_late, 0, 3 * tokens)
-    send_kv(0, 2)
     take_swap(0)
     take_fwd(VALUE)
-    wait_kv(0, 1)
-    attend(head_own)
+    send_kv(0, 2)
     wait_hgt(VALUE, 3)
     project(VALUE, head_late, 0, 3 * tokens)
-    send_kv(1, 2)
     wait_hgt(QUERY, 1, 4)
     project(QUERY, head_beside, 0, tokens)
     take_swap(1)
     attend((head_beside[0], 1))
     take_fwd(QUERY)
+    send_kv(1, 2)
     attend((head_beside[0] + 1, head_beside[1] - 1))
     wait_hgt(QUERY, 2, 5, 3)
     project(QUERY, head_other, 0, tokens)
@@ -420,18 +430,19 @@
         in_specs=[
             pl.BlockSpec(memory_space=pltpu.HBM),
             pl.BlockSpec(memory_space=pltpu.HBM),
-            pl.BlockSpec(memory_space=pltpu.SMEM),
+            pl.BlockSpec(memory_space=pltpu.HBM),
         ],
         out_specs=pl.BlockSpec(memory_space=pltpu.VMEM),
         scratch_shapes=[
+            pltpu.SMEM(tile_mask.shape, jnp.int32),
             pltpu.VMEM((3, frames, rows, columns, features), jnp.bfloat16),
             pltpu.VMEM((3 * count, features), jnp.bfloat16),
             pltpu.VMEM((3, width, features), jnp.bfloat16),
-            pltpu.VMEM((heads, slots * 3 * count, HEAD_DIM), jnp.bfloat16),
-            pltpu.VMEM((heads, slots * 3 * count, HEAD_DIM), jnp.bfloat16),
+            pltpu.VMEM((heads, count // CUBE, slots * 3 * CUBE, HEAD_DIM), jnp.bfloat16),
+            pltpu.VMEM((heads, count // CUBE, slots * 3 * CUBE, HEAD_DIM), jnp.bfloat16),
             pltpu.VMEM((heads, count, HEAD_DIM), jnp.bfloat16),
             pltpu.VMEM((count, slots * 3 * count), jnp.bfloat16),
-            dma((4,)), dma((2, 2)), dma((2, 2)), dma((3, 2, 2)), dma((3, 2, 2)), dma((3, 2)), dma((3, 2)),
+            dma((5,)), dma((2, 2)), dma((2, 2)), dma((3, 2, 2)), dma((3, 2, 2)), dma((3, 2)), dma((3, 2)),
             dma((2,)), dma((2,)), dma((3, 6, n_h - 1)), dma((3, 6, n_h - 1)), dma((2, 3, 2)), dma((2, 3, 2)),
         ],
         compiler_params=pltpu.CompilerParams(

time: 39.2 us -> 38.5 us (0.982)
  Pallas kernels: 38.2 us -> 37.5 us
    pallas_call x1, Pallas kernels: 38.2 us -> 37.5 us  [per_device(): pl.pallas_call(functools.partial(kernel, n_h, n_w), out_shape=jax.ShapeDt...]
where the time goes in v3:
time: 38.5 us; the launch traced here: 38.3 us
  Pallas kernels  37.5 us (97%)
  local copies, waits for them, and re-layouts  0.84 us (2%)
    pallas_call x1, Pallas kernels, per_device(): pl.pallas_call(functools.partial(kernel, n_h, n_w), out_shape=jax.ShapeDt...  37.5 us
    reshape x1, local copies, waits for them, and re-layouts, per_device(): return out.reshape(clips, frames, rows, columns, width)  0.84 us

profile of v3, /device:TPU:0, one launch (start us, length us, event | category | flops | bytes accessed | tf_op | source)
XLA Modules:
  0.0 38.3 jit_solution(17840984932384115267)
XLA Ops:
  0.0 37.5 %shard_map.37 = bf16[256,768]{1,0:T(8,128)(2,1)S(1)} custom-call(bf16[1,16,4,4,1536]{4,3,2,1,0:T(4,128)(2,1)} %x_ref.1, bf16[3,96,1536]{2,1,0:T(8,128)(2,1)} %w_ref.1, s32[1,4,2,4]{3,2,1,0:T(2,128)} %tm_ref.1), custom_call_target="tpu_custom_call" | custom-call | tf_op jit(solution)/shard_map/pallas_call | solution.py:427
  37.5 0.8 %reshape.3 = bf16[1,16,4,4,768]{4,3,2,1,0:T(4,128)(2,1)} reshape(bf16[256,768]{1,0:T(8,128)(2,1)S(1)} %shard_map.37) | data formatting | bytes 786432 | tf_op jit(solution)/shard_map/reshape | solution.py:452

commit v4 on v3

--- a/solution.py
+++ b/solution.py
@@ -270,20 +270,30 @@
 
     def project(s, some, start, length):
         first, count = some
-        place_rows = pl.ds(pl.multiple_of(first * HEAD_DIM, HEAD_DIM), count * HEAD_DIM)
-        raw = lax.dot_general(
-            xn[start : start + length, :], w_all[s, place_rows], contract_last, preferred_element_type=jnp.float32
-        )
-        for j in range(count):
-            part = raw[:, j * HEAD_DIM : (j + 1) * HEAD_DIM]
-            if s == QUERY:
-                qbuf[first + j] = head_norm(part)
-                continue
-            buf = kbuf if s == KEY else vbuf
-            part = head_norm(part) if s == KEY else part.astype(jnp.bfloat16)
-            for t, c, at in blocks:
-                if start <= at < start + length:
-                    buf[first + j, t, c * CUBE : (c + 1) * CUBE, :] = part[at - start : at - start + CUBE]
+        wide = 2 if count % 2 == 0 else 1 if s != QUERY else count
+
+        def body(i, carry):
+            head = first + i * wide
+            place_rows = pl.ds(pl.multiple_of(head * HEAD_DIM, HEAD_DIM), wide * HEAD_DIM)
+            raw = lax.dot_general(
+                xn[start : start + length, :], w_all[s, place_rows], contract_last, preferred_element_type=jnp.float32
+            )
+            for j in range(wide):
+                part = raw[:, j * HEAD_DIM : (j + 1) * HEAD_DIM]
+                if s == QUERY:
+                    qbuf[head + j] = head_norm(part)
+                    continue
+                buf = kbuf if s == KEY else vbuf
+                part = head_norm(part) if s == KEY else part.astype(jnp.bfloat16)
+                for t, c, at in blocks:
+                    if start <= at < start + length:
+                        buf[head + j, t, c * CUBE : (c + 1) * CUBE, :] = part[at - start : at - start + CUBE]
+            return carry
+
+        if count == wide:
+            body(0, 0)
+        else:
+            lax.fori_loop(0, count // wide, body, 0)
 
     def send_kv(which, part):
         @pl.when(has_above)
@@ -371,13 +381,12 @@
     send_kv(0, 2)
     wait_hgt(VALUE, 3)
     project(VALUE, head_late, 0, 3 * tokens)
+    take_swap(1)
+    take_fwd(QUERY)
     wait_hgt(QUERY, 1, 4)
     project(QUERY, head_beside, 0, tokens)
-    take_swap(1)
-    attend((head_beside[0], 1))
-    take_fwd(QUERY)
     send_kv(1, 2)
-    attend((head_beside[0] + 1, head_beside[1] - 1))
+    attend(head_beside)
     wait_hgt(QUERY, 2, 5, 3)
     project(QUERY, head_other, 0, tokens)
     wait_kv(2)

time: 38.5 us -> 37.6 us (0.977)
  Pallas kernels: 37.5 us -> 36.5 us
    pallas_call x1, Pallas kernels: 37.5 us -> 36.5 us  [per_device(): pl.pallas_call(functools.partial(kernel, n_h, n_w), out_shape=jax.ShapeDt...]
where the time goes in v4:
time: 37.6 us; the launch traced here: 37.4 us
  Pallas kernels  36.5 us (97%)
  local copies, waits for them, and re-layouts  0.84 us (2%)
    pallas_call x1, Pallas kernels, per_device(): pl.pallas_call(functools.partial(kernel, n_h, n_w), out_shape=jax.ShapeDt...  36.5 us
    reshape x1, local copies, waits for them, and re-layouts, per_device(): return out.reshape(clips, frames, rows, columns, width)  0.84 us

profile of v4, /device:TPU:0, one launch (start us, length us, event | category | flops | bytes accessed | tf_op | source)
XLA Modules:
  0.0 37.4 jit_solution(12900186305963168725)
XLA Ops:
  0.0 36.5 %shard_map.37 = bf16[256,768]{1,0:T(8,128)(2,1)S(1)} custom-call(bf16[1,16,4,4,1536]{4,3,2,1,0:T(4,128)(2,1)} %x_ref.1, bf16[3,96,1536]{2,1,0:T(8,128)(2,1)} %w_ref.1, s32[1,4,2,4]{3,2,1,0:T(2,128)} %tm_ref.1), custom_call_target="tpu_custom_call" | custom-call | tf_op jit(solution)/shard_map/pallas_call | solution.py:436
  36.6 0.8 %reshape.3 = bf16[1,16,4,4,768]{4,3,2,1,0:T(4,128)(2,1)} reshape(bf16[256,768]{1,0:T(8,128)(2,1)S(1)} %shard_map.37) | data formatting | bytes 786432 | tf_op jit(solution)/shard_map/reshape | solution.py:461

commit v5 on v4

--- a/solution.py
+++ b/solution.py
@@ -372,12 +372,12 @@
     project(VALUE, head_early, early_tokens, late_tokens)
     send_kv(1, 1)
     take_fwd(KEY)
+    wait_hgt(KEY, 3)
+    project(KEY, head_late, 0, 3 * tokens)
+    take_fwd(VALUE)
+    take_swap(0)
     wait_kv(0, 1)
     attend(head_own)
-    wait_hgt(KEY, 3)
-    project(KEY, head_late, 0, 3 * tokens)
-    take_swap(0)
-    take_fwd(VALUE)
     send_kv(0, 2)
     wait_hgt(VALUE, 3)
     project(VALUE, head_late, 0, 3 * tokens)

time: 37.6 us -> 37.5 us (level)
  no operation moved by 1% of the time
where the time goes in v5:
time: 37.5 us; the launch traced here: 37.4 us
  Pallas kernels  36.5 us (97%)
  local copies, waits for them, and re-layouts  0.84 us (2%)
    pallas_call x1, Pallas kernels, per_device(): pl.pallas_call(functools.partial(kernel, n_h, n_w), out_shape=jax.ShapeDt...  36.5 us
    reshape x1, local copies, waits for them, and re-layouts, per_device(): return out.reshape(clips, frames, rows, columns, width)  0.84 us

profile of v5, /device:TPU:0, one launch (start us, length us, event | category | flops | bytes accessed | tf_op | source)
XLA Modules:
  0.0 37.4 jit_solution(11538244736392990380)
XLA Ops:
  0.0 36.5 %shard_map.37 = bf16[256,768]{1,0:T(8,128)(2,1)S(1)} custom-call(bf16[1,16,4,4,1536]{4,3,2,1,0:T(4,128)(2,1)} %x_ref.1, bf16[3,96,1536]{2,1,0:T(8,128)(2,1)} %w_ref.1, s32[1,4,2,4]{3,2,1,0:T(2,128)} %tm_ref.1), custom_call_target="tpu_custom_call" | custom-call | tf_op jit(solution)/shard_map/pallas_call | solution.py:436
  36.6 0.8 %reshape.3 = bf16[1,16,4,4,768]{4,3,2,1,0:T(4,128)(2,1)} reshape(bf16[256,768]{1,0:T(8,128)(2,1)S(1)} %shard_map.37) | data formatting | bytes 786432 | tf_op jit(solution)/shard_map/reshape | solution.py:461
